TPU v7x, 32 devices: a whole 2x2x4 slice. The times are simulated.
32 devices in a mesh: row: 4 (over z), col: 8 (over y, x, core).
Axes of the slice: x: 2, y: 2, z: 4, core: 2. Of those that a mesh axis runs over, the one named last changes fastest.
Arguments:
- velocity: bfloat16 [3, 8, 2048, 2048], P(None, 'col', 'row'), may hold values from -6 to 6
- vorticity: bfloat16 [3, 8, 2048, 2048], P(None, 'col', 'row'), may hold values from -6 to 6
- eddy_state: bfloat16 [8, 64, 3072], P('col', 'row'), may hold values from -0.359375 to 0.359375
- eddy_rate: bfloat16 [8, 64], P('col', 'row'), may hold values from 8 to 64
- block_owner: int32 [8, 4, 64, 1], P('col', 'row'), may hold values from 0 to 3; in each aligned block of 64 rows (0 to 63, 64 to 127, ..., all dimensions but the last counted through in order) at most 32 rows name the same one
- block_slot: int32 [8, 4, 64], P('col', 'row'), may hold values from 0 to 15
Outputs:
- spectral: float32 [3, 8, 1638400], P(None, None, ('row', 'col'))
Inputs may be any that keep to these rules, and one draw needn't show every extreme that they name: `block_owner`: among the 64 blocks of one DNS device, at most 32 have the same owner.
All inputs are finite; a program needn't handle non-finite values.
Results may differ from a plain program's by a relative error of at most 0.013.
Values may be sent and summed in bfloat16 or wider, within the bound.
A program may use at most 128 MiB of HBM per device.

v0:
```python
import math
import jax
import jax.numpy as jnp
from jax import lax
from jax.sharding import PartitionSpec as P

NX = 2048
NY = 2048
KXM = 640
KYM = 1280
RATIO = 4
BY = 8
BX = 128
S = 16
BLKV = 3072
section_step = 0.5
viscous_step = 0.15
vertical_step = 0.5


def padded_2(cells, sides, width):
    for axis, dim in sides:
        count = lax.axis_size(axis)
        head = lax.slice_in_dim(cells, 0, width, axis=dim)
        tail = lax.slice_in_dim(cells, cells.shape[dim] - width, cells.shape[dim], axis=dim)
        cells = jnp.concatenate(
            [
                lax.ppermute(tail, axis, [(i, (i + 1) % count) for i in range(count)]),
                cells,
                lax.ppermute(head, axis, [((i + 1) % count, i) for i in range(count)]),
            ],
            axis=dim,
        )
    return cells


def gauss_value(position, ratio):
    spread = 4.0 * ratio * ratio
    taps = jnp.arange(5 * ratio).astype(jnp.float32)
    shifted = taps - 2.0 * ratio - (ratio - 1) / 2.0
    total = jnp.sum(jnp.exp(-shifted * shifted / (2.0 * spread)))
    moved = position - 2.0 * ratio - (ratio - 1) / 2.0
    return jnp.exp(-moved * moved / (2.0 * spread)) / total


def x_weights(points, coarse, ratio):
    fine = jnp.arange(points, dtype=jnp.int32)[:, None]
    cells = jnp.arange(coarse, dtype=jnp.int32)[None, :]
    offset = jnp.mod(fine - ratio * cells + 2 * ratio, points)
    value = gauss_value(offset.astype(jnp.float32), ratio)
    return jnp.where(offset < 5 * ratio, value, 0.0).astype(jnp.bfloat16)


def y_weights(coarse, padded, ratio):
    cells = jnp.arange(coarse, dtype=jnp.int32)[:, None]
    fine = jnp.arange(padded, dtype=jnp.int32)[None, :]
    offset = fine - ratio * cells
    value = gauss_value(offset.astype(jnp.float32), ratio)
    return jnp.where((offset >= 0) & (offset < 5 * ratio), value, 0.0).astype(jnp.bfloat16)


def x_table(points, kept):
    fine = jnp.arange(points, dtype=jnp.int32)[:, None]
    column = jnp.arange(2 * kept, dtype=jnp.int32)[None, :]
    phase = jnp.mod(column // 2 * fine, points).astype(jnp.float32) * (2.0 * math.pi / points)
    value = jnp.where(column % 2 == 0, jnp.cos(phase), -jnp.sin(phase))
    return (value / math.sqrt(points)).astype(jnp.bfloat16)


def y_tables(points, kept, first, count):
    fine = jnp.arange(points, dtype=jnp.int32)[:, None]
    wave = jnp.arange(count, dtype=jnp.int32)[None, :] + (first - kept // 2)
    phase = jnp.mod(wave * fine, points).astype(jnp.float32) * (2.0 * math.pi / points)
    scale = 1.0 / math.sqrt(points)
    return (
        (jnp.cos(phase) * scale).astype(jnp.bfloat16),
        (jnp.sin(phase) * scale).astype(jnp.bfloat16),
    )


def vertical_inverse(planes):
    index = jnp.arange(planes)
    ends = (index == 0) | (index == planes - 1)
    diagonal = jnp.where(ends, 1.0 + vertical_step, 1.0 + 2.0 * vertical_step).astype(jnp.float32)
    lower = jnp.where(index == 0, 0.0, -vertical_step).astype(jnp.float32)
    upper = jnp.where(index == planes - 1, 0.0, -vertical_step).astype(jnp.float32)
    return lax.linalg.tridiagonal_solve(lower, diagonal, upper, jnp.eye(planes, dtype=jnp.float32))


def damping(x_wave, y_wave, points_x, points_y):
    angle_x = x_wave.astype(jnp.float32) * (2.0 * math.pi / points_x)
    angle_y = y_wave.astype(jnp.float32) * (2.0 * math.pi / points_y)
    total = (
        angle_y[:, None, None] * angle_y[:, None, None]
        + angle_x[None, None, :] * angle_x[None, None, :]
    )
    return jnp.broadcast_to(jnp.exp(-viscous_step * total), (y_wave.shape[0], 2, x_wave.shape[0]))


def along_y(piece):
    items, width, length = piece.shape
    half = width // 2
    split = piece.reshape(items, half, 2, length)
    real_in = split[:, :, 0, :]
    imag_in = split[:, :, 1, :]
    block = 256
    outputs = []
    for first in range(0, KYM, block):
        cosine, sine = y_tables(length, KYM, first, block)
        real_out = jnp.einsum(
            "kin,nj->kji", real_in, cosine, preferred_element_type=jnp.float32
        ) + jnp.einsum("kin,nj->kji", imag_in, sine, preferred_element_type=jnp.float32)
        imag_out = jnp.einsum(
            "kin,nj->kji", imag_in, cosine, preferred_element_type=jnp.float32
        ) - jnp.einsum("kin,nj->kji", real_in, sine, preferred_element_type=jnp.float32)
        outputs.append(jnp.concatenate([real_out, imag_out], axis=2))
    return jnp.concatenate(outputs, axis=1).astype(jnp.bfloat16)


def per_device(velocity, vorticity, eddy_state, eddy_rate, block_owner, block_slot):
    components, depth, rows, points = velocity.shape
    coarse_rows = rows // RATIO
    coarse_cols = points // RATIO
    xweights = x_weights(points, coarse_cols, RATIO)
    local = jnp.einsum(
        "czyn,nx->czyx", velocity, xweights, preferred_element_type=jnp.float32
    ).astype(jnp.bfloat16)
    along = padded_2(local, (("row", 2),), 2 * RATIO)
    yweights = y_weights(coarse_rows, rows + 4 * RATIO, RATIO)
    filtered = jnp.einsum(
        "iy,czyx->czix", yweights, along, preferred_element_type=jnp.float32
    ).astype(jnp.bfloat16)
    ybands = coarse_rows // BY
    xbands = coarse_cols // BX
    count = depth * ybands * xbands
    blocks = filtered.reshape(components, depth, ybands, BY, xbands, BX).transpose(1, 2, 4, 0, 3, 5)
    blocks = blocks.reshape(count, BLKV)
    owners = block_owner.reshape(count)
    slots = block_slot.reshape(count)
    owners_total = lax.axis_size("row")
    every_state, every_rate = (
        lax.all_gather(eddy_state, "row", axis=1, tiled=True),
        lax.all_gather(eddy_rate, "row", axis=1, tiled=True),
    )
    chosen = owners * S + slots
    lookup = (chosen[:, None] == jnp.arange(owners_total * S, dtype=jnp.int32)[None, :]).astype(
        jnp.bfloat16
    )
    state = jnp.dot(lookup, every_state[0], preferred_element_type=jnp.float32)
    rates = jnp.dot(lookup, every_rate[0][:, None], preferred_element_type=jnp.float32)[:, 0]
    forcing_blocks = (rates[:, None] * (state - blocks.astype(jnp.float32))).astype(jnp.bfloat16)
    coarse = forcing_blocks.reshape(depth, ybands, xbands, components, BY, BX).transpose(
        3, 0, 1, 4, 2, 5
    )
    coarse = coarse.reshape(components, depth, coarse_rows, coarse_cols).astype(jnp.float32)
    forcing = jnp.repeat(jnp.repeat(coarse, RATIO, axis=2), RATIO, axis=3)
    speed = velocity.astype(jnp.float32)
    spin = vorticity.astype(jnp.float32)
    cross = jnp.stack(
        [
            speed[1] * spin[2] - speed[2] * spin[1],
            speed[2] * spin[0] - speed[0] * spin[2],
            speed[0] * spin[1] - speed[1] * spin[0],
        ],
        axis=0,
    )
    section = (speed + section_step * (cross + forcing)).astype(jnp.bfloat16)
    xtable = x_table(points, KXM)
    spectrum = jnp.einsum(
        "kyn,nm->kmy",
        section.reshape(components * depth, rows, points),
        xtable,
        preferred_element_type=jnp.float32,
    ).astype(jnp.bfloat16)
    ordered = along_y(lax.all_to_all(spectrum, "row", split_axis=1, concat_axis=2, tiled=True))
    ordered = ordered.reshape(components, depth, KYM, -1)
    inverse = vertical_inverse(depth * lax.axis_size("col")).astype(jnp.bfloat16)
    mode_rows = KYM // lax.axis_size("col")
    mode_cols = ordered.shape[3] // 2
    x_wave = lax.axis_index("row") * mode_cols + jnp.arange(mode_cols, dtype=jnp.int32)
    y_wave = lax.axis_index("col") * mode_rows + jnp.arange(mode_rows, dtype=jnp.int32) - KYM // 2
    factor = damping(x_wave, y_wave, NX, NY).reshape(-1)
    piece = lax.all_to_all(ordered, "col", split_axis=2, concat_axis=1, tiled=True)
    items = piece.shape[0]
    flat = piece.reshape(items, piece.shape[1], -1)
    mixed = jnp.einsum("wz,kzl->kwl", inverse, flat, preferred_element_type=jnp.float32)
    return mixed * factor[None, None, :]


def solution(mesh):
    return jax.shard_map(
        per_device,
        mesh=mesh,
        in_specs=(
            P(None, "col", "row", None),
            P(None, "col", "row", None),
            P("col", "row", None),
            P("col", "row"),
            P("col", "row", None, None),
            P("col", "row", None),
        ),
        out_specs=P(None, None, ("row", "col")),
        check_vma=False,
    )
```

profile of v0, /device:TPU:0, one launch (start us, length us, event | category | flops | bytes accessed | tf_op | source)
XLA Modules:
  0.0 582.2 jit_solution(14752560193493699065)
XLA Ops:
  0.7 8.0 %fusion.97 = bf16[3,1,512,512]{3,2,0,1:T(8,128)(2,1)S(1)} fusion(bf16[3,1,512,2048]{3,2,1,0:T(8,128)(2,1)} %param.6, f32[]{:T(128)} %fusion.202, s32[512]{0:T(512)S(1)} %iota_multiply_fusion), kind=kOutput, calls=%fused_computation.125 | convolution fusion | flops 3245080576 | bytes 7866372 | tf_op jit(solution)/shard_map/czyn,nx->czyx/dot_general | solution.py:125
  8.7 3.1 collective-permute-start
  13.9 8.7 %copy.30 = bf16[3,1,512,2048]{2,3,0,1:T(8,128)(2,1)} copy(bf16[3,1,512,2048]{3,2,1,0:T(8,128)(2,1)} %param.6) | data formatting | bytes 12582912 | tf_op args[0]
  24.1 10.3 %all-reduce = bf16[64]{0:T(256)(128)(2,1)S(1)} all-reduce(bf16[64]{0:T(256)(128)(2,1)S(1)} %dynamic-update-slice), channel_id=1, replica_groups=mesh['row'=4,'col'=8] {'row'}, use_global_device_ids=true, to_apply=%add | all-reduce | flops 64 | bytes 256 | tf_op jit(solution)/shard_map/reshape
  34.4 14.6 %all_gather.7 = bf16[1,64,3072]{2,1,0:T(8,128)(2,1)S(1)} all-gather(bf16[1,16,3072]{2,1,0:T(8,128)(2,1)S(1)} %copy-done.1), channel_id=1, replica_groups=mesh['row'=4,'col'=8] {'row'}, dimensions={1}, use_global_device_ids=true | all-gather | bytes 491520 | tf_op jit(solution)/shard_map/all_gather | solution.py:142
  49.1 9.2 %convert_element_type.226 = f32[3,1,512,2048]{2,3,0,1:T(8,128)} convert(bf16[3,1,512,2048]{2,3,0,1:T(8,128)(2,1)} %copy.30) | non-fusion elementwise | flops 3145728 | bytes 18874368 | tf_op jit(solution)/shard_map/convert_element_type | solution.py:157
  58.3 8.6 %copy.31 = bf16[3,1,512,2048]{2,3,0,1:T(8,128)(2,1)} copy(bf16[3,1,512,2048]{3,2,1,0:T(8,128)(2,1)} %param.7) | data formatting | bytes 12582912 | tf_op args[1]
  66.8 9.7 %convert_element_type.227 = f32[3,1,512,2048]{2,3,0,1:T(8,128)} convert(bf16[3,1,512,2048]{2,3,0,1:T(8,128)(2,1)} %copy.31) | non-fusion elementwise | flops 3145728 | bytes 18874368 | tf_op jit(solution)/shard_map/convert_element_type | solution.py:158
  76.7 10.0 %multiply_subtract_fusion.2 = (f32[1,1,512,2048]{2,3,0,1:T(8,128)}, f32[1,1,512,2048]{2,3,0,1:T(8,128)}, f32[1,1,512,2048]{2,3,0,1:T(8,128)}) fusion(f32[3,1,512,2048]{2,3,0,1:T(8,128)} %convert_element_type.227, f32[3,1,512,2048]{2,3,0,1:T(8,128)S(1)} %copy-done), kind=kLoop, calls=%fused_computation.41 | loop fusion | flops 9437184 | bytes 37748736 | tf_op jit(solution)/shard_map/sub | solution.py:161
  86.8 45.1 %fusion.364 = bf16[2048,1280,1]{0,1,2:T(8,128)(2,1)} fusion(s32[1280]{0:T(1024)S(1)} %add_select_fusion.7, pred[1280]{0:T(1024)(128)(4,1)S(1)} %fusion.192), kind=kLoop, calls=%fused_computation.25.clone.clone.clone.clone.clone.clone.2 | loop fusion | flops 47185920 | bytes 5249280 | tf_op jit(solution)/shard_map/kyn,nm->kmy/dot_general | solution.py:169
  136.6 3.2 broadcast_in_dim.46
  142.2 7.7 %broadcast_in_dim.47 = f32[3,512,512,4]{1,3,2,0:T(4,128)} broadcast(f32[3,512,512]{1,2,0:T(8,128)} %copy.35), dimensions={0,1,2} | broadcast | bytes 15728640 | tf_op jit(solution)/shard_map/broadcast_in_dim | solution.py:156
  149.9 14.7 %broadcast_in_dim.48 = f32[3,1,512,2048]{2,3,0,1:T(8,128)} reshape(f32[3,512,512,4]{1,3,2,0:T(4,128)} %broadcast_in_dim.47) | data formatting | bytes 25165824 | tf_op jit(solution)/shard_map/broadcast_in_dim | solution.py:156
  164.5 17.5 %fusion.36 = bf16[3,1280,512]{2,1,0:T(8,128)(2,1)S(1)} fusion(f32[3,1,512,2048]{2,3,0,1:T(8,128)} %broadcast_in_dim.48, f32[1,1,512,2048]{2,3,0,1:T(8,128)} %get-tuple-element.22, f32[1,1,512,2048]{2,3,0,1:T(8,128)} %get-tuple-element.21, f32[1,1,512,2048]{2,3,0,1:T(8,128)} %get-tuple-element.20, bf16[3,1,512,2048]{2,3,0,1:T(8,128)(2,1)} %copy.30, ...), kind=kOutput, calls=%fused_computation.44 | convolution fusion | flops 8077049856 | bytes 40632320 | tf_op jit(solution)/shard_map/kyn,nm->kmy/dot_general | solution.py:169
  182.0 17.5 %copy.37 = bf16[3,1280,512]{2,0,1:T(4,128)(2,1)} copy(bf16[3,1280,512]{2,1,0:T(8,128)(2,1)S(1)} %fusion.36) | data formatting | bytes 7864320 | tf_op jit(solution)/shard_map/convert_element_type | solution.py:174
  199.5 5.1 all-to-all-start
  204.6 111.3 %all-to-all-done = bf16[3,1280,512]{2,0,1:T(4,128)(2,1)} async-done(((bf16[3,1280,512]{2,0,1:T(4,128)(2,1)}), bf16[3,1280,512]{2,0,1:T(4,128)(2,1)}, u32[]{:S(2)}, u32[]{:S(2)}) %all-to-all-start) | async-done | bytes 3932192 | tf_op jit(solution)/shard_map/all_to_all | solution.py:175
  315.9 8.1 %copy.51 = bf16[3,4,320,512]{3,1,2,0:T(4,128)(2,1)} copy(bf16[3,4,320,512]{3,0,2,1:T(4,128)(2,1)} %bitcast.24) | data formatting | bytes 7864320 | tf_op jit(solution)/shard_map/all_to_all | solution.py:175
  324.0 10.0 %reshape.376 = bf16[3,160,2,2048]{3,2,1,0:T(2,128)(2,1)} reshape(bf16[3,320,4,512]{3,2,1,0:T(4,128)(2,1)} %bitcast.237) | data formatting | bytes 7864320 | tf_op jit(solution)/shard_map/reshape | solution.py:103
  334.0 8.6 %fusion.332 = (bf16[3,160,1,2048]{3,2,1,0:T(2,128)(2,1)S(1)}, bf16[3,160,1,2048]{3,2,1,0:T(2,128)(2,1)S(1)}) fusion(bf16[3,160,2,2048]{3,2,1,0:T(2,128)(2,1)} %reshape.376), kind=kLoop, calls=%fused_computation.391 | loop fusion | bytes 7864320 | tf_op jit(solution)/shard_map/slice | solution.py:104
  342.6 2.5 copy_bitcast_fusion.1
  345.1 8.0 %fusion.165 = f32[256,3,160]{0,2,1:T(8,128)S(1)} fusion(bf16[3,160,2048]{2,1,0:T(8,128)(2,1)S(1)} %get-tuple-element.53, s32[256]{0:T(256)S(1)} %iota_add_fusion.4), kind=kOutput, calls=%fused_computation.181 | convolution fusion | flops 511705088 | bytes 2458624 | tf_op jit(solution)/shard_map/kin,nj->kji/dot_general | solution.py:110
  353.1 8.2 %fusion.163 = f32[256,3,160]{0,2,1:T(8,128)S(1)} fusion(bf16[3,160,2048]{2,1,0:T(8,128)(2,1)S(1)} %get-tuple-element.52, s32[256]{0:T(256)S(1)} %iota_add_fusion.4), kind=kOutput, calls=%fused_computation.180 | convolution fusion | flops 511705088 | bytes 2458624 | tf_op jit(solution)/shard_map/kin,nj->kji/dot_general | solution.py:113
  361.3 8.4 %fusion.159 = f32[256,3,160]{0,2,1:T(8,128)S(1)} fusion(bf16[3,160,2048]{2,1,0:T(8,128)(2,1)S(1)} %get-tuple-element.53, s32[256]{0:T(256)S(1)} %iota_add_fusion.3), kind=kOutput, calls=%fused_computation.179 | convolution fusion | flops 511705088 | bytes 2458624 | tf_op jit(solution)/shard_map/kin,nj->kji/dot_general | solution.py:110
  369.7 8.1 %fusion.157 = f32[256,3,160]{0,2,1:T(8,128)S(1)} fusion(bf16[3,160,2048]{2,1,0:T(8,128)(2,1)S(1)} %get-tuple-element.52, s32[256]{0:T(256)S(1)} %iota_add_fusion.3), kind=kOutput, calls=%fused_computation.178 | convolution fusion | flops 511705088 | bytes 2458624 | tf_op jit(solution)/shard_map/kin,nj->kji/dot_general | solution.py:113
  377.8 8.0 %fusion.153 = f32[256,3,160]{0,2,1:T(8,128)S(1)} fusion(bf16[3,160,2048]{2,1,0:T(8,128)(2,1)S(1)} %get-tuple-element.53, s32[256]{0:T(256)S(1)} %iota_add_fusion.2), kind=kOutput, calls=%fused_computation.177 | convolution fusion | flops 511705088 | bytes 2458624 | tf_op jit(solution)/shard_map/kin,nj->kji/dot_general | solution.py:110
  385.8 8.2 %fusion.151 = f32[256,3,160]{0,2,1:T(8,128)S(1)} fusion(bf16[3,160,2048]{2,1,0:T(8,128)(2,1)S(1)} %get-tuple-element.52, s32[256]{0:T(256)S(1)} %iota_add_fusion.2), kind=kOutput, calls=%fused_computation.176 | convolution fusion | flops 511705088 | bytes 2458624 | tf_op jit(solution)/shard_map/kin,nj->kji/dot_general | solution.py:113
  394.0 8.4 %fusion.147 = f32[256,3,160]{0,2,1:T(8,128)S(1)} fusion(bf16[3,160,2048]{2,1,0:T(8,128)(2,1)S(1)} %get-tuple-element.53, s32[256]{0:T(256)S(1)} %iota_add_fusion.1), kind=kOutput, calls=%fused_computation.175 | convolution fusion | flops 511705088 | bytes 2458624 | tf_op jit(solution)/shard_map/kin,nj->kji/dot_general | solution.py:110
  402.4 8.0 %fusion.145 = f32[256,3,160]{0,2,1:T(8,128)S(1)} fusion(bf16[3,160,2048]{2,1,0:T(8,128)(2,1)S(1)} %get-tuple-element.52, s32[256]{0:T(256)S(1)} %iota_add_fusion.1), kind=kOutput, calls=%fused_computation.174 | convolution fusion | flops 511705088 | bytes 2458624 | tf_op jit(solution)/shard_map/kin,nj->kji/dot_general | solution.py:113
  410.4 8.1 %fusion.141 = f32[256,3,160]{0,2,1:T(8,128)S(1)} fusion(bf16[3,160,2048]{2,1,0:T(8,128)(2,1)S(1)} %get-tuple-element.53, s32[256]{0:T(256)S(1)} %iota_add_fusion), kind=kOutput, calls=%fused_computation.173 | convolution fusion | flops 511705088 | bytes 2458624 | tf_op jit(solution)/shard_map/kin,nj->kji/dot_general | solution.py:110
  418.5 8.2 %fusion.139 = f32[256,3,160]{0,2,1:T(8,128)S(1)} fusion(bf16[3,160,2048]{2,1,0:T(8,128)(2,1)S(1)} %get-tuple-element.52, s32[256]{0:T(256)S(1)} %iota_add_fusion), kind=kOutput, calls=%fused_computation.172 | convolution fusion | flops 511705088 | bytes 2458624 | tf_op jit(solution)/shard_map/kin,nj->kji/dot_general | solution.py:113
  426.7 8.6 %fusion.126 = bf16[3,256,160]{1,2,0:T(8,128)(2,1)S(1)} fusion(f32[256,3,160]{0,2,1:T(8,128)S(1)} %fusion.165, bf16[3,160,2048]{2,1,0:T(8,128)(2,1)S(1)} %get-tuple-element.52, s32[256]{0:T(256)S(1)} %iota_add_fusion.4), kind=kOutput, calls=%fused_computation.160 | convolution fusion | flops 511950848 | bytes 2704384 | tf_op jit(solution)/shard_map/kin,nj->kji/dot_general | solution.py:112
  435.3 8.5 %fusion.125 = bf16[3,256,160]{1,2,0:T(8,128)(2,1)S(1)} fusion(f32[256,3,160]{0,2,1:T(8,128)S(1)} %fusion.163, bf16[3,160,2048]{2,1,0:T(8,128)(2,1)S(1)} %get-tuple-element.53, s32[256]{0:T(256)S(1)} %iota_add_fusion.4), kind=kOutput, calls=%fused_computation.159 | convolution fusion | flops 511950848 | bytes 2704384 | tf_op jit(solution)/shard_map/kin,nj->kji/dot_general | solution.py:115
  443.8 9.0 %fusion.124 = bf16[3,256,160]{1,2,0:T(8,128)(2,1)S(1)} fusion(f32[256,3,160]{0,2,1:T(8,128)S(1)} %fusion.159, bf16[3,160,2048]{2,1,0:T(8,128)(2,1)S(1)} %get-tuple-element.52, s32[256]{0:T(256)S(1)} %iota_add_fusion.3), kind=kOutput, calls=%fused_computation.158 | convolution fusion | flops 511950848 | bytes 2704384 | tf_op jit(solution)/shard_map/kin,nj->kji/dot_general | solution.py:112
  452.8 8.5 %fusion.123 = bf16[3,256,160]{1,2,0:T(8,128)(2,1)S(1)} fusion(f32[256,3,160]{0,2,1:T(8,128)S(1)} %fusion.157, bf16[3,160,2048]{2,1,0:T(8,128)(2,1)S(1)} %get-tuple-element.53, s32[256]{0:T(256)S(1)} %iota_add_fusion.3), kind=kOutput, calls=%fused_computation.157 | convolution fusion | flops 511950848 | bytes 2704384 | tf_op jit(solution)/shard_map/kin,nj->kji/dot_general | solution.py:115
  461.3 8.7 %fusion.122 = bf16[3,256,160]{1,2,0:T(8,128)(2,1)S(1)} fusion(f32[256,3,160]{0,2,1:T(8,128)S(1)} %fusion.153, bf16[3,160,2048]{2,1,0:T(8,128)(2,1)S(1)} %get-tuple-element.52, s32[256]{0:T(256)S(1)} %iota_add_fusion.2), kind=kOutput, calls=%fused_computation.156 | convolution fusion | flops 511950848 | bytes 2704384 | tf_op jit(solution)/shard_map/kin,nj->kji/dot_general | solution.py:112
  470.0 8.5 %fusion.121 = bf16[3,256,160]{1,2,0:T(8,128)(2,1)S(1)} fusion(f32[256,3,160]{0,2,1:T(8,128)S(1)} %fusion.151, bf16[3,160,2048]{2,1,0:T(8,128)(2,1)S(1)} %get-tuple-element.53, s32[256]{0:T(256)S(1)} %iota_add_fusion.2), kind=kOutput, calls=%fused_computation.155 | convolution fusion | flops 511950848 | bytes 2704384 | tf_op jit(solution)/shard_map/kin,nj->kji/dot_general | solution.py:115
  478.5 8.8 %fusion.120 = bf16[3,256,160]{1,2,0:T(8,128)(2,1)S(1)} fusion(f32[256,3,160]{0,2,1:T(8,128)S(1)} %fusion.147, bf16[3,160,2048]{2,1,0:T(8,128)(2,1)S(1)} %get-tuple-element.52, s32[256]{0:T(256)S(1)} %iota_add_fusion.1), kind=kOutput, calls=%fused_computation.154 | convolution fusion | flops 511950848 | bytes 2704384 | tf_op jit(solution)/shard_map/kin,nj->kji/dot_general | solution.py:112
  487.3 8.5 %fusion.119 = bf16[3,256,160]{1,2,0:T(8,128)(2,1)S(1)} fusion(f32[256,3,160]{0,2,1:T(8,128)S(1)} %fusion.145, bf16[3,160,2048]{2,1,0:T(8,128)(2,1)S(1)} %get-tuple-element.53, s32[256]{0:T(256)S(1)} %iota_add_fusion.1), kind=kOutput, calls=%fused_computation.153 | convolution fusion | flops 511950848 | bytes 2704384 | tf_op jit(solution)/shard_map/kin,nj->kji/dot_general | solution.py:115
  495.8 8.8 %fusion.118 = bf16[3,256,160]{1,2,0:T(8,128)(2,1)S(1)} fusion(f32[256,3,160]{0,2,1:T(8,128)S(1)} %fusion.141, bf16[3,160,2048]{2,1,0:T(8,128)(2,1)S(1)} %get-tuple-element.52, s32[256]{0:T(256)S(1)} %iota_add_fusion), kind=kOutput, calls=%fused_computation.152 | convolution fusion | flops 511950848 | bytes 2704384 | tf_op jit(solution)/shard_map/kin,nj->kji/dot_general | solution.py:112
  504.7 8.5 %fusion.117 = bf16[3,256,160]{1,2,0:T(8,128)(2,1)S(1)} fusion(f32[256,3,160]{0,2,1:T(8,128)S(1)} %fusion.139, bf16[3,160,2048]{2,1,0:T(8,128)(2,1)S(1)} %get-tuple-element.53, s32[256]{0:T(256)S(1)} %iota_add_fusion), kind=kOutput, calls=%fused_computation.151 | convolution fusion | flops 511950848 | bytes 2704384 | tf_op jit(solution)/shard_map/kin,nj->kji/dot_general | solution.py:115
  513.4 6.0 %copy.41 = bf16[3,1,1280,320]{3,0,1,2:T(4,128)(2,1)} copy(bf16[3,1,1280,320]{2,3,0,1:T(8,128)(2,1)S(1)} %fusion.171) | data formatting | bytes 4915200 | tf_op jit(solution)/shard_map/concatenate | solution.py:117
  519.4 4.8 all-to-all-start.1
  540.7 5.0 fusion.328
  545.9 24.7 %all-to-all-done.1 = bf16[3,1,1280,320]{3,0,1,2:T(4,128)(2,1)} async-done(((bf16[3,1,1280,320]{3,0,1,2:T(4,128)(2,1)}), bf16[3,1,1280,320]{3,0,1,2:T(4,128)(2,1)}, u32[]{:S(2)}, u32[]{:S(2)}) %all-to-all-start.1) | async-done | bytes 2457632 | tf_op jit(solution)/shard_map/all_to_all | solution.py:183
  570.5 2.5 copy.42
  573.1 3.9 reshape.377
  577.0 4.7 fusion
  (61 shorter events, 13.8 us)
Async XLA Ops:
  8.7 123.2 %collective-permute-start = (bf16[3,1,8,512]{3,2,0,1:T(8,128)(2,1)S(1)}, bf16[3,1,8,512]{3,2,0,1:T(8,128)(2,1)S(1)}, u32[]{:S(2)}, u32[]{:S(2)}) collective-permute-start(bf16[3,1,8,512]{3,2,0,1:T(8,128)(2,1)S(1)} %get-tuple-element.25), channel_id=1, source_target_pairs={{0,8},{8,16},{16,24},{24,0},{1,9},{9,17},{17,25},{25,1},{2,10},{10... | collective-permute-start | bytes 73736 | tf_op jit(solution)/shard_map/ppermute | solution.py:28
  11.8 120.1 %collective-permute-start.1 = (bf16[3,1,8,512]{3,2,0,1:T(8,128)(2,1)S(1)}, bf16[3,1,8,512]{3,2,0,1:T(8,128)(2,1)S(1)}, u32[]{:S(2)}, u32[]{:S(2)}) collective-permute-start(bf16[3,1,8,512]{3,2,0,1:T(8,128)(2,1)S(1)} %get-tuple-element.26), channel_id=1, source_target_pairs={{8,0},{16,8},{24,16},{0,24},{9,1},{17,9},{25,17},{1,25},{10,2},{18... | collective-permute-start | bytes 73736 | tf_op jit(solution)/shard_map/ppermute | solution.py:30
  13.9 8.7 %copy-start.5 = (u32[32]{0:T(128)S(1)}, u32[32]{0:T(128)}, u32[]{:S(2)}) copy-start(u32[32]{0:T(128)} %constant.167) | copy-start | bytes 388
  13.9 10.0 %copy-start.2 = (bf16[1,16]{1,0:T(2,128)(2,1)S(1)}, bf16[1,16]{1,0:T(2,128)(2,1)}, u32[]{:S(2)}) copy-start(bf16[1,16]{1,0:T(2,128)(2,1)} %param.9) | copy-start | bytes 100
  13.9 20.6 %copy-start.1 = (bf16[1,16,3072]{2,1,0:T(8,128)(2,1)S(1)}, bf16[1,16,3072]{2,1,0:T(8,128)(2,1)}, u32[]{:S(2)}) copy-start(bf16[1,16,3072]{2,1,0:T(8,128)(2,1)} %param.8) | copy-start | bytes 294916
  66.8 9.7 %copy-start.3 = (s32[1,1,64]{2,1,0:T(1,128)S(1)}, s32[1,1,64]{2,1,0:T(1,128)}, u32[]{:S(2)}) copy-start(s32[1,1,64]{2,1,0:T(1,128)} %param.11) | copy-start | bytes 772
  66.8 9.7 %copy-start.4 = (s32[1,1,64,1]{2,3,1,0:T(1,128)S(1)}, s32[1,1,64,1]{2,3,1,0:T(1,128)}, u32[]{:S(2)}) copy-start(s32[1,1,64,1]{2,3,1,0:T(1,128)} %param.10) | copy-start | bytes 772
  66.8 9.9 %copy-start = (f32[3,1,512,2048]{2,3,0,1:T(8,128)S(1)}, f32[3,1,512,2048]{2,3,0,1:T(8,128)}, u32[]{:S(2)}) copy-start(f32[3,1,512,2048]{2,3,0,1:T(8,128)} %convert_element_type.226) | copy-start | bytes 37748740
  199.5 116.4 %all-to-all-start = ((bf16[3,1280,512]{2,0,1:T(4,128)(2,1)}), bf16[3,1280,512]{2,0,1:T(4,128)(2,1)}, u32[]{:S(2)}, u32[]{:S(2)}) async-start(bf16[3,1280,512]{2,0,1:T(4,128)(2,1)} %copy.37), calls=%async_computation | async-start | bytes 10485760 | tf_op jit(solution)/shard_map/all_to_all | solution.py:175
  519.4 51.1 %all-to-all-start.1 = ((bf16[3,1,1280,320]{3,0,1,2:T(4,128)(2,1)}), bf16[3,1,1280,320]{3,0,1,2:T(4,128)(2,1)}, u32[]{:S(2)}, u32[]{:S(2)}) async-start(bf16[3,1,1280,320]{3,0,1,2:T(4,128)(2,1)} %copy.41), calls=%async_computation.1 | async-start | bytes 7864320 | tf_op jit(solution)/shard_map/all_to_all | solution.py:183
where the time goes:
time: 589 us; the launch traced here: 582 us
  matrix products  200 us (34%)
  waiting for transfers between devices  136 us (23%)
  local copies, waits for them, and re-layouts  111 us (19%)
  other arithmetic  80.1 us (14%)
  blocking collectives  24.9 us (4%)
  between operations  15.4 us (3%)
  starting transfers between devices  15.1 us (3%)
    all_to_all x1, waiting for transfers between devices, per_device(): lax.all_to_all(spectrum, 'row', split_axis=1, concat_axis=2, tiled=True)  111 us
    dot_general x1, other arithmetic, per_device(): jnp.einsum('kyn,nm->kmy', section.reshape(components * depth, rows, point...  45.1 us
    dot_general x5, matrix products, along_y(): jnp.einsum('kin,nj->kji', imag_in, sine, preferred_element_type=jnp.float32)  43.9 us
    dot_general x5, matrix products, along_y(): jnp.einsum('kin,nj->kji', real_in, sine, preferred_element_type=jnp.float32)  42.5 us
    dot_general x5, matrix products, along_y(): jnp.einsum('kin,nj->kji', real_in, cosine, preferred_element_type=jnp.flo...  40.9 us
    dot_general x5, matrix products, along_y(): jnp.einsum('kin,nj->kji', imag_in, cosine, preferred_element_type=jnp.flo...  40.7 us
    broadcast_in_dim x5, local copies, waits for them, and re-layouts, per_device(): forcing = jnp.repeat(jnp.repeat(coarse, RATIO, axis=2), RATIO, axis=3)  30.2 us
    all_to_all x1, waiting for transfers between devices, per_device(): lax.all_to_all(ordered, 'col', split_axis=2, concat_axis=1, tiled=True)  24.7 us
  transfers between devices with their start and end apart: 4, of which 2 were waited for; matrix products, arithmetic and copies ran while one was open for 17% of the time, Pallas kernels for 0%

commit v1 on v0

--- a/solution.py
+++ b/solution.py
@@ -172,7 +172,14 @@
         xtable,
         preferred_element_type=jnp.float32,
     ).astype(jnp.bfloat16)
-    ordered = along_y(lax.all_to_all(spectrum, "row", split_axis=1, concat_axis=2, tiled=True))
+    ordered = along_y(
+        jnp.concatenate(
+            lax.all_to_all(
+                jnp.stack(jnp.split(spectrum, lax.axis_size("row"), axis=1)), "row", 0, 0
+            ),
+            axis=2,
+        )
+    )
     ordered = ordered.reshape(components, depth, KYM, -1)
     inverse = vertical_inverse(depth * lax.axis_size("col")).astype(jnp.bfloat16)
     mode_rows = KYM // lax.axis_size("col")

time: 589 us -> 544 us (0.924)
  waiting for transfers between devices: 136 us -> 108 us
  local copies, waits for them, and re-layouts: 111 us -> 92.6 us
    all_to_all x1, waiting for transfers between devices: 111 us -> 83.2 us  [per_device(): lax.all_to_all(jnp.stack(jnp.split(spectrum, lax.axis_size('row'), axis=1...]
    convert_element_type x1 -> x0, local copies, waits for them, and re-layouts: 17.5 us -> none  [per_device(): spectrum = jnp.einsum('kyn,nm->kmy', section.reshape(components * depth,...]
    another operation x0 -> x2, local copies, waits for them, and re-layouts: none -> 10.5 us  [the longest x1 9.99 us: along_y(): split = piece.reshape(items, half, 2, length)]
    all_to_all x1 -> x0, local copies, waits for them, and re-layouts: 8.12 us -> none  [per_device(): lax.all_to_all(spectrum, 'row', split_axis=1, concat_axis=2, tiled=True)]
  transfers between devices with their start and end apart: 4 -> 4, of which waited for: 2 -> 2; matrix products, arithmetic and copies ran while one was open for 17% -> 19% of each run, Pallas kernels for 0% -> 0%
where the time goes in v1:
time: 544 us; the launch traced here: 538 us
  matrix products  200 us (37%)
  waiting for transfers between devices  108 us (20%)
  local copies, waits for them, and re-layouts  92.6 us (17%)
  other arithmetic  82.3 us (15%)
  blocking collectives  24.9 us (5%)
  between operations  15.5 us (3%)
  starting transfers between devices  14.8 us (3%)
    all_to_all x1, waiting for transfers between devices, per_device(): lax.all_to_all(jnp.stack(jnp.split(spectrum, lax.axis_size('row'), axis=1...  83.2 us
    dot_general x1, other arithmetic, per_device(): jnp.einsum('kyn,nm->kmy', section.reshape(components * depth, rows, point...  45.1 us
    dot_general x5, matrix products, along_y(): jnp.einsum('kin,nj->kji', imag_in, sine, preferred_element_type=jnp.float32)  43.9 us
    dot_general x5, matrix products, along_y(): jnp.einsum('kin,nj->kji', real_in, sine, preferred_element_type=jnp.float32)  42.5 us
    dot_general x5, matrix products, along_y(): jnp.einsum('kin,nj->kji', real_in, cosine, preferred_element_type=jnp.flo...  40.9 us
    dot_general x5, matrix products, along_y(): jnp.einsum('kin,nj->kji', imag_in, cosine, preferred_element_type=jnp.flo...  40.7 us
    broadcast_in_dim x5, local copies, waits for them, and re-layouts, per_device(): forcing = jnp.repeat(jnp.repeat(coarse, RATIO, axis=2), RATIO, axis=3)  30.2 us
    all_to_all x1, waiting for transfers between devices, per_device(): lax.all_to_all(ordered, 'col', split_axis=2, concat_axis=1, tiled=True)  24.6 us
  transfers between devices with their start and end apart: 4, of which 2 were waited for; matrix products, arithmetic and copies ran while one was open for 19% of the time, Pallas kernels for 0%

profile of v1, /device:TPU:0, one launch (start us, length us, event | category | flops | bytes accessed | tf_op | source)
XLA Modules:
  0.0 537.9 jit_solution(12512847664156099405)
XLA Ops:
  0.7 8.0 %fusion.97 = bf16[3,1,512,512]{3,2,0,1:T(8,128)(2,1)S(1)} fusion(bf16[3,1,512,2048]{3,2,1,0:T(8,128)(2,1)} %param.6, f32[]{:T(128)} %fusion.202, s32[512]{0:T(512)S(1)} %iota_multiply_fusion), kind=kOutput, calls=%fused_computation.125 | convolution fusion | flops 3245080576 | bytes 7866372 | tf_op jit(solution)/shard_map/czyn,nx->czyx/dot_general | solution.py:125
  8.7 3.1 collective-permute-start
  13.9 8.7 %copy.30 = bf16[3,1,512,2048]{2,3,0,1:T(8,128)(2,1)} copy(bf16[3,1,512,2048]{3,2,1,0:T(8,128)(2,1)} %param.6) | data formatting | bytes 12582912 | tf_op args[0]
  24.1 10.3 %all-reduce = bf16[64]{0:T(256)(128)(2,1)S(1)} all-reduce(bf16[64]{0:T(256)(128)(2,1)S(1)} %dynamic-update-slice), channel_id=1, replica_groups=mesh['row'=4,'col'=8] {'row'}, use_global_device_ids=true, to_apply=%add | all-reduce | flops 64 | bytes 256 | tf_op jit(solution)/shard_map/reshape
  34.4 14.6 %all_gather.7 = bf16[1,64,3072]{2,1,0:T(8,128)(2,1)S(1)} all-gather(bf16[1,16,3072]{2,1,0:T(8,128)(2,1)S(1)} %copy-done.1), channel_id=1, replica_groups=mesh['row'=4,'col'=8] {'row'}, dimensions={1}, use_global_device_ids=true | all-gather | bytes 491520 | tf_op jit(solution)/shard_map/all_gather | solution.py:142
  49.0 9.2 %convert_element_type.226 = f32[3,1,512,2048]{2,3,0,1:T(8,128)} convert(bf16[3,1,512,2048]{2,3,0,1:T(8,128)(2,1)} %copy.30) | non-fusion elementwise | flops 3145728 | bytes 18874368 | tf_op jit(solution)/shard_map/convert_element_type | solution.py:157
  58.2 8.6 %copy.31 = bf16[3,1,512,2048]{2,3,0,1:T(8,128)(2,1)} copy(bf16[3,1,512,2048]{3,2,1,0:T(8,128)(2,1)} %param.7) | data formatting | bytes 12582912 | tf_op args[1]
  66.8 9.7 %convert_element_type.227 = f32[3,1,512,2048]{2,3,0,1:T(8,128)} convert(bf16[3,1,512,2048]{2,3,0,1:T(8,128)(2,1)} %copy.31) | non-fusion elementwise | flops 3145728 | bytes 18874368 | tf_op jit(solution)/shard_map/convert_element_type | solution.py:158
  76.8 10.0 %multiply_subtract_fusion.2 = (f32[1,1,512,2048]{2,3,0,1:T(8,128)}, f32[1,1,512,2048]{2,3,0,1:T(8,128)}, f32[1,1,512,2048]{2,3,0,1:T(8,128)}) fusion(f32[3,1,512,2048]{2,3,0,1:T(8,128)} %convert_element_type.227, f32[3,1,512,2048]{2,3,0,1:T(8,128)S(1)} %copy-done), kind=kLoop, calls=%fused_computation.41 | loop fusion | flops 9437184 | bytes 37748736 | tf_op jit(solution)/shard_map/sub | solution.py:161
  86.8 45.1 %fusion.364 = bf16[2048,1280,1]{0,1,2:T(8,128)(2,1)} fusion(s32[1280]{0:T(1024)S(1)} %add_select_fusion.7, pred[1280]{0:T(1024)(128)(4,1)S(1)} %fusion.192), kind=kLoop, calls=%fused_computation.25.clone.clone.clone.clone.clone.clone.2 | loop fusion | flops 47185920 | bytes 5249280 | tf_op jit(solution)/shard_map/kyn,nm->kmy/dot_general | solution.py:169
  136.6 3.2 broadcast_in_dim.46
  139.8 2.4 copy.35
  142.2 7.7 %broadcast_in_dim.47 = f32[3,512,512,4]{1,3,2,0:T(4,128)} broadcast(f32[3,512,512]{1,2,0:T(8,128)} %copy.35), dimensions={0,1,2} | broadcast | bytes 15728640 | tf_op jit(solution)/shard_map/broadcast_in_dim | solution.py:156
  149.9 14.7 %broadcast_in_dim.48 = f32[3,1,512,2048]{2,3,0,1:T(8,128)} reshape(f32[3,512,512,4]{1,3,2,0:T(4,128)} %broadcast_in_dim.47) | data formatting | bytes 25165824 | tf_op jit(solution)/shard_map/broadcast_in_dim | solution.py:156
  164.5 17.4 %fusion.36 = bf16[3,1280,512]{2,1,0:T(8,128)(2,1)S(1)} fusion(f32[3,1,512,2048]{2,3,0,1:T(8,128)} %broadcast_in_dim.48, f32[1,1,512,2048]{2,3,0,1:T(8,128)} %get-tuple-element.22, f32[1,1,512,2048]{2,3,0,1:T(8,128)} %get-tuple-element.21, f32[1,1,512,2048]{2,3,0,1:T(8,128)} %get-tuple-element.20, bf16[3,1,512,2048]{2,3,0,1:T(8,128)(2,1)} %copy.30, ...), kind=kOutput, calls=%fused_computation.44 | convolution fusion | flops 8077049856 | bytes 40632320 | tf_op jit(solution)/shard_map/kyn,nm->kmy/dot_general | solution.py:169
  184.6 4.8 all-to-all-start
  189.5 83.2 %all-to-all-done = bf16[4,3,320,512]{3,2,1,0:T(8,128)(2,1)} async-done(((bf16[4,3,320,512]{3,2,1,0:T(8,128)(2,1)}), bf16[4,3,320,512]{3,2,1,0:T(8,128)(2,1)}, u32[]{:S(2)}, u32[]{:S(2)}) %all-to-all-start) | async-done | bytes 3932192 | tf_op jit(solution)/shard_map/all_to_all | solution.py:177
  272.7 7.1 %copy.37 = bf16[3,320,4,512]{3,2,1,0:T(4,128)(2,1)} copy(bf16[3,320,4,512]{3,1,0,2:T(8,128)(2,1)} %bitcast.28) | data formatting | bytes 7864320 | tf_op jit(solution)/shard_map/reshape | solution.py:176
  279.8 10.0 %reshape_reshape.3 = bf16[3,160,2,2048]{3,2,1,0:T(2,128)(2,1)} reshape(bf16[3,320,4,512]{3,2,1,0:T(4,128)(2,1)} %copy.37) | data formatting | bytes 7864320 | tf_op jit(solution)/shard_map/reshape;reshape | solution.py:103
  289.8 8.5 %fusion.332 = (bf16[3,160,1,2048]{3,2,1,0:T(2,128)(2,1)S(1)}, bf16[3,160,1,2048]{3,2,1,0:T(2,128)(2,1)S(1)}) fusion(bf16[3,160,2,2048]{3,2,1,0:T(2,128)(2,1)} %reshape_reshape.3), kind=kLoop, calls=%fused_computation.395 | loop fusion | bytes 7864320 | tf_op jit(solution)/shard_map/slice | solution.py:104
  298.3 2.5 copy_bitcast_fusion
  300.8 8.0 %fusion.141 = f32[256,3,160]{0,2,1:T(8,128)S(1)} fusion(bf16[3,160,2048]{2,1,0:T(8,128)(2,1)S(1)} %get-tuple-element.57, s32[256]{0:T(256)S(1)} %iota_add_fusion), kind=kOutput, calls=%fused_computation.173 | convolution fusion | flops 511705088 | bytes 2458624 | tf_op jit(solution)/shard_map/kin,nj->kji/dot_general | solution.py:110
  308.8 8.2 %fusion.139 = f32[256,3,160]{0,2,1:T(8,128)S(1)} fusion(bf16[3,160,2048]{2,1,0:T(8,128)(2,1)S(1)} %get-tuple-element.56, s32[256]{0:T(256)S(1)} %iota_add_fusion), kind=kOutput, calls=%fused_computation.172 | convolution fusion | flops 511705088 | bytes 2458624 | tf_op jit(solution)/shard_map/kin,nj->kji/dot_general | solution.py:113
  317.0 8.4 %fusion.147 = f32[256,3,160]{0,2,1:T(8,128)S(1)} fusion(bf16[3,160,2048]{2,1,0:T(8,128)(2,1)S(1)} %get-tuple-element.57, s32[256]{0:T(256)S(1)} %iota_add_fusion.1), kind=kOutput, calls=%fused_computation.175 | convolution fusion | flops 511705088 | bytes 2458624 | tf_op jit(solution)/shard_map/kin,nj->kji/dot_general | solution.py:110
  325.4 8.1 %fusion.145 = f32[256,3,160]{0,2,1:T(8,128)S(1)} fusion(bf16[3,160,2048]{2,1,0:T(8,128)(2,1)S(1)} %get-tuple-element.56, s32[256]{0:T(256)S(1)} %iota_add_fusion.1), kind=kOutput, calls=%fused_computation.174 | convolution fusion | flops 511705088 | bytes 2458624 | tf_op jit(solution)/shard_map/kin,nj->kji/dot_general | solution.py:113
  333.5 8.0 %fusion.153 = f32[256,3,160]{0,2,1:T(8,128)S(1)} fusion(bf16[3,160,2048]{2,1,0:T(8,128)(2,1)S(1)} %get-tuple-element.57, s32[256]{0:T(256)S(1)} %iota_add_fusion.2), kind=kOutput, calls=%fused_computation.177 | convolution fusion | flops 511705088 | bytes 2458624 | tf_op jit(solution)/shard_map/kin,nj->kji/dot_general | solution.py:110
  341.5 8.2 %fusion.151 = f32[256,3,160]{0,2,1:T(8,128)S(1)} fusion(bf16[3,160,2048]{2,1,0:T(8,128)(2,1)S(1)} %get-tuple-element.56, s32[256]{0:T(256)S(1)} %iota_add_fusion.2), kind=kOutput, calls=%fused_computation.176 | convolution fusion | flops 511705088 | bytes 2458624 | tf_op jit(solution)/shard_map/kin,nj->kji/dot_general | solution.py:113
  349.7 8.4 %fusion.159 = f32[256,3,160]{0,2,1:T(8,128)S(1)} fusion(bf16[3,160,2048]{2,1,0:T(8,128)(2,1)S(1)} %get-tuple-element.57, s32[256]{0:T(256)S(1)} %iota_add_fusion.3), kind=kOutput, calls=%fused_computation.179 | convolution fusion | flops 511705088 | bytes 2458624 | tf_op jit(solution)/shard_map/kin,nj->kji/dot_general | solution.py:110
  358.1 8.0 %fusion.157 = f32[256,3,160]{0,2,1:T(8,128)S(1)} fusion(bf16[3,160,2048]{2,1,0:T(8,128)(2,1)S(1)} %get-tuple-element.56, s32[256]{0:T(256)S(1)} %iota_add_fusion.3), kind=kOutput, calls=%fused_computation.178 | convolution fusion | flops 511705088 | bytes 2458624 | tf_op jit(solution)/shard_map/kin,nj->kji/dot_general | solution.py:113
  366.1 8.1 %fusion.165 = f32[256,3,160]{0,2,1:T(8,128)S(1)} fusion(bf16[3,160,2048]{2,1,0:T(8,128)(2,1)S(1)} %get-tuple-element.57, s32[256]{0:T(256)S(1)} %iota_add_fusion.4), kind=kOutput, calls=%fused_computation.181 | convolution fusion | flops 511705088 | bytes 2458624 | tf_op jit(solution)/shard_map/kin,nj->kji/dot_general | solution.py:110
  374.2 8.2 %fusion.163 = f32[256,3,160]{0,2,1:T(8,128)S(1)} fusion(bf16[3,160,2048]{2,1,0:T(8,128)(2,1)S(1)} %get-tuple-element.56, s32[256]{0:T(256)S(1)} %iota_add_fusion.4), kind=kOutput, calls=%fused_computation.180 | convolution fusion | flops 511705088 | bytes 2458624 | tf_op jit(solution)/shard_map/kin,nj->kji/dot_general | solution.py:113
  382.4 8.6 %fusion.118 = bf16[3,256,160]{1,2,0:T(8,128)(2,1)S(1)} fusion(f32[256,3,160]{0,2,1:T(8,128)S(1)} %fusion.141, bf16[3,160,2048]{2,1,0:T(8,128)(2,1)S(1)} %get-tuple-element.56, s32[256]{0:T(256)S(1)} %iota_add_fusion), kind=kOutput, calls=%fused_computation.152 | convolution fusion | flops 511950848 | bytes 2704384 | tf_op jit(solution)/shard_map/kin,nj->kji/dot_general | solution.py:112
  391.0 8.5 %fusion.117 = bf16[3,256,160]{1,2,0:T(8,128)(2,1)S(1)} fusion(f32[256,3,160]{0,2,1:T(8,128)S(1)} %fusion.139, bf16[3,160,2048]{2,1,0:T(8,128)(2,1)S(1)} %get-tuple-element.57, s32[256]{0:T(256)S(1)} %iota_add_fusion), kind=kOutput, calls=%fused_computation.151 | convolution fusion | flops 511950848 | bytes 2704384 | tf_op jit(solution)/shard_map/kin,nj->kji/dot_general | solution.py:115
  399.5 9.0 %fusion.120 = bf16[3,256,160]{1,2,0:T(8,128)(2,1)S(1)} fusion(f32[256,3,160]{0,2,1:T(8,128)S(1)} %fusion.147, bf16[3,160,2048]{2,1,0:T(8,128)(2,1)S(1)} %get-tuple-element.56, s32[256]{0:T(256)S(1)} %iota_add_fusion.1), kind=kOutput, calls=%fused_computation.154 | convolution fusion | flops 511950848 | bytes 2704384 | tf_op jit(solution)/shard_map/kin,nj->kji/dot_general | solution.py:112
  408.5 8.5 %fusion.119 = bf16[3,256,160]{1,2,0:T(8,128)(2,1)S(1)} fusion(f32[256,3,160]{0,2,1:T(8,128)S(1)} %fusion.145, bf16[3,160,2048]{2,1,0:T(8,128)(2,1)S(1)} %get-tuple-element.57, s32[256]{0:T(256)S(1)} %iota_add_fusion.1), kind=kOutput, calls=%fused_computation.153 | convolution fusion | flops 511950848 | bytes 2704384 | tf_op jit(solution)/shard_map/kin,nj->kji/dot_general | solution.py:115
  417.0 8.7 %fusion.122 = bf16[3,256,160]{1,2,0:T(8,128)(2,1)S(1)} fusion(f32[256,3,160]{0,2,1:T(8,128)S(1)} %fusion.153, bf16[3,160,2048]{2,1,0:T(8,128)(2,1)S(1)} %get-tuple-element.56, s32[256]{0:T(256)S(1)} %iota_add_fusion.2), kind=kOutput, calls=%fused_computation.156 | convolution fusion | flops 511950848 | bytes 2704384 | tf_op jit(solution)/shard_map/kin,nj->kji/dot_general | solution.py:112
  425.7 8.5 %fusion.121 = bf16[3,256,160]{1,2,0:T(8,128)(2,1)S(1)} fusion(f32[256,3,160]{0,2,1:T(8,128)S(1)} %fusion.151, bf16[3,160,2048]{2,1,0:T(8,128)(2,1)S(1)} %get-tuple-element.57, s32[256]{0:T(256)S(1)} %iota_add_fusion.2), kind=kOutput, calls=%fused_computation.155 | convolution fusion | flops 511950848 | bytes 2704384 | tf_op jit(solution)/shard_map/kin,nj->kji/dot_general | solution.py:115
  434.2 8.8 %fusion.124 = bf16[3,256,160]{1,2,0:T(8,128)(2,1)S(1)} fusion(f32[256,3,160]{0,2,1:T(8,128)S(1)} %fusion.159, bf16[3,160,2048]{2,1,0:T(8,128)(2,1)S(1)} %get-tuple-element.56, s32[256]{0:T(256)S(1)} %iota_add_fusion.3), kind=kOutput, calls=%fused_computation.158 | convolution fusion | flops 511950848 | bytes 2704384 | tf_op jit(solution)/shard_map/kin,nj->kji/dot_general | solution.py:112
  443.0 8.5 %fusion.123 = bf16[3,256,160]{1,2,0:T(8,128)(2,1)S(1)} fusion(f32[256,3,160]{0,2,1:T(8,128)S(1)} %fusion.157, bf16[3,160,2048]{2,1,0:T(8,128)(2,1)S(1)} %get-tuple-element.57, s32[256]{0:T(256)S(1)} %iota_add_fusion.3), kind=kOutput, calls=%fused_computation.157 | convolution fusion | flops 511950848 | bytes 2704384 | tf_op jit(solution)/shard_map/kin,nj->kji/dot_general | solution.py:115
  451.5 8.8 %fusion.126 = bf16[3,256,160]{1,2,0:T(8,128)(2,1)S(1)} fusion(f32[256,3,160]{0,2,1:T(8,128)S(1)} %fusion.165, bf16[3,160,2048]{2,1,0:T(8,128)(2,1)S(1)} %get-tuple-element.56, s32[256]{0:T(256)S(1)} %iota_add_fusion.4), kind=kOutput, calls=%fused_computation.160 | convolution fusion | flops 511950848 | bytes 2704384 | tf_op jit(solution)/shard_map/kin,nj->kji/dot_general | solution.py:112
  460.4 8.5 %fusion.125 = bf16[3,256,160]{1,2,0:T(8,128)(2,1)S(1)} fusion(f32[256,3,160]{0,2,1:T(8,128)S(1)} %fusion.163, bf16[3,160,2048]{2,1,0:T(8,128)(2,1)S(1)} %get-tuple-element.57, s32[256]{0:T(256)S(1)} %iota_add_fusion.4), kind=kOutput, calls=%fused_computation.159 | convolution fusion | flops 511950848 | bytes 2704384 | tf_op jit(solution)/shard_map/kin,nj->kji/dot_general | solution.py:115
  469.1 6.0 %copy.40 = bf16[3,1,1280,320]{3,0,1,2:T(4,128)(2,1)} copy(bf16[3,1,1280,320]{2,3,0,1:T(8,128)(2,1)S(1)} %fusion.171) | data formatting | bytes 4915200 | tf_op jit(solution)/shard_map/concatenate | solution.py:117
  475.1 4.8 all-to-all-start.1
  496.6 5.0 fusion.328
  501.7 24.6 %all-to-all-done.1 = bf16[3,1,1280,320]{3,0,1,2:T(4,128)(2,1)} async-done(((bf16[3,1,1280,320]{3,0,1,2:T(4,128)(2,1)}), bf16[3,1,1280,320]{3,0,1,2:T(4,128)(2,1)}, u32[]{:S(2)}, u32[]{:S(2)}) %all-to-all-start.1) | async-done | bytes 2457632 | tf_op jit(solution)/shard_map/all_to_all | solution.py:190
  526.2 2.5 copy.41
  528.7 3.9 reshape.376
  532.7 4.7 fusion
  (62 shorter events, 14.1 us)
Async XLA Ops:
  8.7 123.2 %collective-permute-start = (bf16[3,1,8,512]{3,2,0,1:T(8,128)(2,1)S(1)}, bf16[3,1,8,512]{3,2,0,1:T(8,128)(2,1)S(1)}, u32[]{:S(2)}, u32[]{:S(2)}) collective-permute-start(bf16[3,1,8,512]{3,2,0,1:T(8,128)(2,1)S(1)} %get-tuple-element.29), channel_id=1, source_target_pairs={{0,8},{8,16},{16,24},{24,0},{1,9},{9,17},{17,25},{25,1},{2,10},{10... | collective-permute-start | bytes 73736 | tf_op jit(solution)/shard_map/ppermute | solution.py:28
  11.8 120.1 %collective-permute-start.1 = (bf16[3,1,8,512]{3,2,0,1:T(8,128)(2,1)S(1)}, bf16[3,1,8,512]{3,2,0,1:T(8,128)(2,1)S(1)}, u32[]{:S(2)}, u32[]{:S(2)}) collective-permute-start(bf16[3,1,8,512]{3,2,0,1:T(8,128)(2,1)S(1)} %get-tuple-element.30), channel_id=1, source_target_pairs={{8,0},{16,8},{24,16},{0,24},{9,1},{17,9},{25,17},{1,25},{10,2},{18... | collective-permute-start | bytes 73736 | tf_op jit(solution)/shard_map/ppermute | solution.py:30
  13.9 8.7 %copy-start.5 = (u32[32]{0:T(128)S(1)}, u32[32]{0:T(128)}, u32[]{:S(2)}) copy-start(u32[32]{0:T(128)} %constant.167) | copy-start | bytes 388
  13.9 10.0 %copy-start.2 = (bf16[1,16]{1,0:T(2,128)(2,1)S(1)}, bf16[1,16]{1,0:T(2,128)(2,1)}, u32[]{:S(2)}) copy-start(bf16[1,16]{1,0:T(2,128)(2,1)} %param.9) | copy-start | bytes 100
  13.9 20.5 %copy-start.1 = (bf16[1,16,3072]{2,1,0:T(8,128)(2,1)S(1)}, bf16[1,16,3072]{2,1,0:T(8,128)(2,1)}, u32[]{:S(2)}) copy-start(bf16[1,16,3072]{2,1,0:T(8,128)(2,1)} %param.8) | copy-start | bytes 294916
  66.8 9.7 %copy-start.3 = (s32[1,1,64]{2,1,0:T(1,128)S(1)}, s32[1,1,64]{2,1,0:T(1,128)}, u32[]{:S(2)}) copy-start(s32[1,1,64]{2,1,0:T(1,128)} %param.11) | copy-start | bytes 772
  66.8 9.7 %copy-start.4 = (s32[1,1,64,1]{2,3,1,0:T(1,128)S(1)}, s32[1,1,64,1]{2,3,1,0:T(1,128)}, u32[]{:S(2)}) copy-start(s32[1,1,64,1]{2,3,1,0:T(1,128)} %param.10) | copy-start | bytes 772
  66.8 9.9 %copy-start = (f32[3,1,512,2048]{2,3,0,1:T(8,128)S(1)}, f32[3,1,512,2048]{2,3,0,1:T(8,128)}, u32[]{:S(2)}) copy-start(f32[3,1,512,2048]{2,3,0,1:T(8,128)} %convert_element_type.226) | copy-start | bytes 37748740
  184.6 88.1 %all-to-all-start = ((bf16[4,3,320,512]{3,2,1,0:T(8,128)(2,1)}), bf16[4,3,320,512]{3,2,1,0:T(8,128)(2,1)}, u32[]{:S(2)}, u32[]{:S(2)}) async-start(bf16[4,3,320,512]{3,2,1,0:T(8,128)(2,1)} %pad_maximum_fusion), calls=%async_computation | async-start | bytes 7864320 | tf_op jit(solution)/shard_map/all_to_all | solution.py:177
  475.1 51.1 %all-to-all-start.1 = ((bf16[3,1,1280,320]{3,0,1,2:T(4,128)(2,1)}), bf16[3,1,1280,320]{3,0,1,2:T(4,128)(2,1)}, u32[]{:S(2)}, u32[]{:S(2)}) async-start(bf16[3,1,1280,320]{3,0,1,2:T(4,128)(2,1)} %copy.40), calls=%async_computation.1 | async-start | bytes 7864320 | tf_op jit(solution)/shard_map/all_to_all | solution.py:190
